TPU v7x, 32 devices: a whole 2x2x4 slice. The times are simulated.
32 devices in a mesh: row: 8 (over z, x), ch: 4 (over y, core).
Axes of the slice: x: 2, y: 2, z: 4, core: 2. Of those that a mesh axis runs over, the one named last changes fastest.
Arguments:
- pair_rep: bfloat16 [128, 8, 8], P('ch', 'row'), may hold values from -6 to 6
- residue_mask: int32 [8], replicated, may hold values 0 or 1
- chain_ids: int32 [8], replicated, may hold values from 0 to 3, never falling along the last dimension, each value on 1 to 4 neighbouring positions
- in_gain: float32 [2, 128], replicated, may hold values from 0.5 to 1.5
- in_bias: float32 [2, 128], replicated, may hold values from -3 to 3
- w_proj: bfloat16 [2, 128, 4, 128], P(None, None, None, 'ch'), may hold values from -0.5 to 0.5
- w_gate: bfloat16 [2, 128, 128], P(None, None, 'ch'), may hold values from -0.5 to 0.5
- pair_bias: float32 [2, 128], P(None, 'ch'), may hold values from -4 to 4
- out_gain: float32 [2, 128], P(None, 'ch'), may hold values from 0.5 to 1.5
- out_bias: float32 [2, 128], P(None, 'ch'), may hold values from -3 to 3
- w_out: bfloat16 [2, 128, 128], P(None, 'ch'), may hold values from -0.5 to 0.5
Outputs:
- pair_out: bfloat16 [128, 8, 8], P('ch', 'row')
Inputs may be any that keep to these rules, and one draw needn't show every extreme that they name: `chain_ids`: chain numbers never fall along the residues; each chain has 1 to 4 residues.
All inputs are finite; a program needn't handle non-finite values.
Results may differ from a plain program's by a relative error of at most 0.013.
Values may be sent and summed in bfloat16 or wider, within the bound.
A program may use at most 64 MiB of HBM per device.

v0:
```python
import jax
import jax.numpy as jnp
from jax import lax
from jax.sharding import PartitionSpec as P

epsilon = 1e-05


def channel_norm(values, norm_gain, norm_bias):
    mean_val = jnp.mean(values, axis=0)
    variance = jnp.mean(values * values, axis=0) - mean_val * mean_val
    return (values - mean_val) * lax.rsqrt(variance + epsilon) * norm_gain[
        :, None, None
    ] + norm_bias[:, None, None]


def prepare(
    pair_local, layer, in_gain, in_bias, w_proj, w_gate, pair_bias, mask_rows, mask_cols, same_chain
):
    full_pair = lax.all_gather(pair_local, "ch", axis=0, tiled=True)
    normed = channel_norm(full_pair.astype(jnp.float32), in_gain[layer], in_bias[layer]).astype(
        jnp.bfloat16
    )
    projected = jnp.einsum(
        "cij,cpd->pdij", normed, w_proj[layer], preferred_element_type=jnp.float32
    )
    pair_mask = mask_rows[:, None] * mask_cols[None, :]
    first_arm = (jax.nn.sigmoid(projected[0]) * projected[1] * pair_mask).astype(jnp.bfloat16)
    second_arm = (jax.nn.sigmoid(projected[2]) * projected[3] * pair_mask).astype(jnp.bfloat16)
    logits = jnp.einsum("cij,cd->dij", normed, w_gate[layer], preferred_element_type=jnp.float32)
    logits = logits + pair_bias[layer][:, None, None] * same_chain[None]
    return (first_arm, second_arm, jax.nn.sigmoid(logits))


def finish(product_sum, gating, layer, out_gain, out_bias, w_out):
    totals = lax.psum(
        (jnp.sum(product_sum, axis=0), jnp.sum(product_sum * product_sum, axis=0)), "ch"
    )
    channels = product_sum.shape[0] * lax.axis_size("ch")
    mean_val = totals[0] / channels
    variance = totals[1] / channels - mean_val * mean_val
    scaled = (product_sum - mean_val) * lax.rsqrt(variance + epsilon)
    normed = (scaled * out_gain[layer][:, None, None] + out_bias[layer][:, None, None]).astype(
        jnp.bfloat16
    )
    columns = w_out[layer]
    mixed = lax.psum_scatter(
        jnp.einsum("dij,dc->cij", normed, columns, preferred_element_type=jnp.float32).astype(
            jnp.bfloat16
        ),
        "ch",
        scatter_dimension=0,
        tiled=True,
    ).astype(jnp.float32)
    return gating * mixed


def body(
    pair_rep,
    residue_mask,
    chain_ids,
    in_gain,
    in_bias,
    w_proj,
    w_gate,
    pair_bias,
    out_gain,
    out_bias,
    w_out,
):
    rows_here = pair_rep.shape[1]
    row_start = lax.axis_index("row") * rows_here
    mask_cols = residue_mask.astype(jnp.float32)
    mask_rows = lax.dynamic_slice_in_dim(mask_cols, row_start, rows_here)
    chain_rows = lax.dynamic_slice_in_dim(chain_ids, row_start, rows_here)
    same_chain = (chain_rows[:, None] == chain_ids[None, :]).astype(jnp.float32)
    first_arm, second_arm, gating = prepare(
        pair_rep, 0, in_gain, in_bias, w_proj, w_gate, pair_bias, mask_rows, mask_cols, same_chain
    )
    product_sum = jnp.einsum(
        "cik,cjk->cij",
        first_arm,
        lax.all_gather(second_arm, "row", axis=1, tiled=True),
        preferred_element_type=jnp.float32,
    )
    middle = (
        pair_rep.astype(jnp.float32) + finish(product_sum, gating, 0, out_gain, out_bias, w_out)
    ).astype(jnp.bfloat16)
    in_first, in_second, in_gating = prepare(
        middle, 1, in_gain, in_bias, w_proj, w_gate, pair_bias, mask_rows, mask_cols, same_chain
    )
    exchanged_left = lax.all_to_all(in_first, "row", split_axis=2, concat_axis=1, tiled=True)
    left_rows = jnp.swapaxes(exchanged_left, 1, 2)
    in_product = jnp.einsum(
        "cik,ckj->cij",
        left_rows,
        lax.all_gather(in_second, "row", axis=1, tiled=True),
        preferred_element_type=jnp.float32,
    )
    update = finish(in_product, in_gating, 1, out_gain, out_bias, w_out)
    return (middle.astype(jnp.float32) + update).astype(jnp.bfloat16)


def solution(mesh):
    return jax.shard_map(
        body,
        mesh=mesh,
        in_specs=(
            P("ch", "row", None),
            P(),
            P(),
            P(),
            P(),
            P(None, None, None, "ch"),
            P(None, None, "ch"),
            P(None, "ch"),
            P(None, "ch"),
            P(None, "ch"),
            P(None, "ch", None),
        ),
        out_specs=P("ch", "row", None),
        check_vma=False,
    )
```

profile of v0, /device:TPU:0, one launch (start us, length us, event | category | flops | bytes accessed | tf_op | source)
XLA Modules:
  0.0 143.6 jit_solution(11897451887013223469)
XLA Ops:
  6.5 0.8 copy.22
  7.3 6.2 %all_gather.12 = bf16[128,1,8]{2,1,0:T(2,128)(2,1)S(1)} all-gather(bf16[32,1,8]{2,1,0:T(2,128)(2,1)S(1)} %copy.22), channel_id=1, replica_groups=mesh['row'=8,'ch'=4] {'ch'}, dimensions={0}, use_global_device_ids=true | all-gather | bytes 2560 | tf_op jit(solution)/shard_map/all_gather | solution.py:20
  13.8 0.6 copy-done.9
  14.4 0.6 dynamic_slice.7
  15.0 0.6 broadcast_multiply_fusion
  15.7 0.6 copy-done.2
  16.7 27.0 %all_gather.13 = bf16[32,8,8]{0,2,1:T(8,128)(2,1)S(1)} all-gather(bf16[32,1,8]{0,2,1:T(8,128)(2,1)S(1)} %fusion.56), channel_id=1, replica_groups=mesh['row'=8,'ch'=4] {'row'}, dimensions={1}, use_global_device_ids=true | all-gather | bytes 4608 | tf_op jit(solution)/shard_map/all_gather | solution.py:83
  43.8 5.7 %all-reduce.1 = (f32[1,8]{1,0:T(1,128)S(1)}, f32[1,8]{1,0:T(1,128)S(1)}) all-reduce(f32[1,8]{1,0:T(1,128)S(1)} %bitcast.174, f32[1,8]{1,0:T(1,128)S(1)} %bitcast.173), channel_id=1, replica_groups=mesh['row'=8,'ch'=4] {'ch'}, use_global_device_ids=true, to_apply=%region_5.0 | all-reduce | flops 16 | bytes 128 | tf_op jit(solution)/shard_map/psum | solution.py:36
  49.5 0.7 copy-done.4
  50.4 0.7 copy.40
  51.1 0.6 copy-done.10
  51.7 0.6 dynamic_slice.6
  52.4 0.6 compare_convert_fusion
  53.1 17.3 %reduce-scatter.7.cloned.1.call-done = bf16[32,8]{1,0:T(8,128)(2,1)} async-done(((bf16[128,8]{1,0:T(8,128)(2,1)}), bf16[32,8]{1,0:T(8,128)(2,1)}) %reduce-scatter.7.cloned.1.call-update) | async-done | bytes 528
  70.4 0.8 copy.41
  71.5 5.2 %all_gather.14 = bf16[128,1,8]{2,1,0:T(2,128)(2,1)S(1)} all-gather(bf16[32,1,8]{2,1,0:T(2,128)(2,1)S(1)} %copy.24), channel_id=1, replica_groups=mesh['row'=8,'ch'=4] {'ch'}, dimensions={0}, use_global_device_ids=true | all-gather | bytes 2560 | tf_op jit(solution)/shard_map/all_gather | solution.py:20
  77.2 0.6 copy.26
  77.9 5.5 %all-to-all-start = ((bf16[32,1,8]{0,1,2:T(2,128)(2,1)}), bf16[32,1,8]{0,1,2:T(2,128)(2,1)S(1)}, u32[]{:S(2)}, u32[]{:S(2)}) async-start(bf16[32,1,8]{0,1,2:T(2,128)(2,1)} %copy.26), calls=%async_computation | async-start | bytes 8192 | tf_op jit(solution)/shard_map/all_to_all | solution.py:92
  83.4 26.6 %all_gather.15 = bf16[32,8,8]{0,2,1:T(8,128)(2,1)S(1)} all-gather(bf16[32,1,8]{0,2,1:T(8,128)(2,1)S(1)} %get-tuple-element.18), channel_id=1, replica_groups=mesh['row'=8,'ch'=4] {'row'}, dimensions={1}, use_global_device_ids=true | all-gather | bytes 4608 | tf_op jit(solution)/shard_map/all_gather | solution.py:97
  110.2 5.9 %all-reduce = (f32[1,8]{1,0:T(1,128)S(1)}, f32[1,8]{1,0:T(1,128)S(1)}) all-reduce(f32[1,8]{1,0:T(1,128)S(1)} %bitcast.176, f32[1,8]{1,0:T(1,128)S(1)} %bitcast.175), channel_id=1, replica_groups=mesh['row'=8,'ch'=4] {'ch'}, use_global_device_ids=true, to_apply=%region_12.0 | all-reduce | flops 16 | bytes 128 | tf_op jit(solution)/shard_map/psum | solution.py:36
  116.4 0.7 copy.42
  117.1 18.1 %reduce-scatter.9.cloned.1.call-done = bf16[32,8]{1,0:T(8,128)(2,1)} async-done(((bf16[128,8]{1,0:T(8,128)(2,1)}), bf16[32,8]{1,0:T(8,128)(2,1)}) %reduce-scatter.9.cloned.1.call-update) | async-done | bytes 528
  135.2 0.8 copy.43
  136.0 0.8 fusion.16
  (49 shorter events, 2.3 us)
Async XLA Ops:
  6.5 63.9 %reduce-scatter.7.cloned.1.call-start = ((), (), s32[]{:S(2)}) async-start(), calls=%async_computation.3 | async-start | bytes 40960
  13.5 2.8 %copy-start.6 = (bf16[2,128,4,32]{1,3,2,0:T(8,128)(2,1)S(1)}, bf16[2,128,4,32]{1,3,2,0:T(8,128)(2,1)}, u32[]{:S(2)}) copy-start(bf16[2,128,4,32]{1,3,2,0:T(8,128)(2,1)} %param.16) | copy-start | bytes 196612
  13.8 0.7 copy-start.9
  15.7 0.7 copy-start.2
  15.7 0.7 copy-start.3
  43.7 6.5 %copy-start.7 = (bf16[2,32,128]{2,1,0:T(8,128)(2,1)S(1)}, bf16[2,32,128]{2,1,0:T(8,128)(2,1)}, u32[]{:S(2)}) copy-start(bf16[2,32,128]{2,1,0:T(8,128)(2,1)} %param.21) | copy-start | bytes 49156
  49.5 0.7 copy-start.4
  49.5 0.7 copy-start.5
  51.1 0.7 copy-start.10
  51.7 0.7 copy-start.1
  51.7 19.4 %copy-start.8 = (bf16[2,128,32]{1,2,0:T(8,128)(2,1)S(1)}, bf16[2,128,32]{1,2,0:T(8,128)(2,1)}, u32[]{:S(2)}) copy-start(bf16[2,128,32]{1,2,0:T(8,128)(2,1)} %param.17) | copy-start | bytes 49156
  53.1 18.1 %copy-start = (bf16[32,1,8]{0,2,1:T(8,128)(2,1)S(1)}, bf16[32,1,8]{0,2,1:T(8,128)(2,1)}, u32[]{:S(2)}) copy-start(bf16[32,1,8]{0,2,1:T(8,128)(2,1)} %param.11) | copy-start | bytes 1540
  77.9 32.2 %all-to-all-start = ((bf16[32,1,8]{0,1,2:T(2,128)(2,1)}), bf16[32,1,8]{0,1,2:T(2,128)(2,1)S(1)}, u32[]{:S(2)}, u32[]{:S(2)}) async-start(bf16[32,1,8]{0,1,2:T(2,128)(2,1)} %copy.26), calls=%async_computation | async-start | bytes 8192 | tf_op jit(solution)/shard_map/all_to_all | solution.py:92
  83.4 51.9 %reduce-scatter.9.cloned.1.call-start = ((), (), s32[]{:S(2)}) async-start(), calls=%async_computation.4 | async-start | bytes 40960
Sparse Core Ops, SparseCore 0:
  51.2 19.1 reduce-scatter.6
  117.2 17.9 reduce-scatter.8
where the time goes:
time: 144 us
  blocking collectives  76.7 us (53%)
  waiting for transfers between devices  35.5 us (25%)
  between operations  13.5 us (9%)
  local copies, waits for them, and re-layouts  8.5 us (6%)
  starting transfers between devices  5.55 us (4%)
  other arithmetic  2.19 us (2%)
  matrix products  1.71 us (1%)
    unnamed x4, waiting for transfers between devices  35.5 us
    all_gather x1, blocking collectives, body(): lax.all_gather(second_arm, 'row', axis=1, tiled=True)  27 us
    all_gather x1, blocking collectives, body(): lax.all_gather(in_second, 'row', axis=1, tiled=True)  26.6 us
    psum x2, blocking collectives, finish(): lax.psum((jnp.sum(product_sum, axis=0), jnp.sum(product_sum * product_sum...  11.6 us
    all_gather x2, blocking collectives, prepare(): full_pair = lax.all_gather(pair_local, 'ch', axis=0, tiled=True)  11.5 us
    unnamed x27, local copies, waits for them, and re-layouts  6.47 us
    all_to_all x1, starting transfers between devices, body(): lax.all_to_all(in_first, 'row', split_axis=2, concat_axis=1, tiled=True)  5.51 us
  transfers between devices with their start and end apart: 3, of which 2 were waited for; matrix products, arithmetic and copies ran while one was open for 1% of the time, Pallas kernels for 0%

commit v1 on v0

--- a/solution.py
+++ b/solution.py
@@ -17,7 +17,12 @@
 def prepare(
     pair_local, layer, in_gain, in_bias, w_proj, w_gate, pair_bias, mask_rows, mask_cols, same_chain
 ):
-    full_pair = lax.all_gather(pair_local, "ch", axis=0, tiled=True)
+    ring = [pair_local]
+    for hop in range(3):
+        ring.append(lax.ppermute(ring[-1], "ch", [(dev, (dev + 1) % 4) for dev in range(4)]))
+    full_pair = jnp.roll(
+        jnp.concatenate(ring[::-1], axis=0), (lax.axis_index("ch") + 1) * ring[0].shape[0], axis=0
+    )
     normed = channel_norm(full_pair.astype(jnp.float32), in_gain[layer], in_bias[layer]).astype(
         jnp.bfloat16
     )

time: 144 us -> 149 us (1.035)
  waiting for transfers between devices: 35.5 us -> 48.1 us
  blocking collectives: 76.7 us -> 65.3 us
  starting transfers between devices: 5.55 us -> 9.05 us
    all_gather x2 -> x0, blocking collectives: 11.5 us -> none  [prepare(): full_pair = lax.all_gather(pair_local, 'ch', axis=0, tiled=True)]
    ppermute x0 -> x6, waiting for transfers between devices: none -> 11.3 us  [prepare(): lax.ppermute(ring[-1], 'ch', [(dev, (dev + 1) % 4) for dev in range(4)])]
    ppermute x0 -> x6, starting transfers between devices: none -> 3.5 us  [prepare(): lax.ppermute(ring[-1], 'ch', [(dev, (dev + 1) % 4) for dev in range(4)])]
    unnamed x27 -> x26, local copies, waits for them, and re-layouts: 6.47 us -> 5.75 us
  transfers between devices with their start and end apart: 3 -> 9, of which waited for: 2 -> 7; matrix products, arithmetic and copies ran while one was open for 1% -> 2% of each run, Pallas kernels for 0% -> 0%
where the time goes in v1:
time: 149 us; the launch traced here: 148 us
  blocking collectives  65.3 us (44%)
  waiting for transfers between devices  48.1 us (32%)
  between operations  13.5 us (9%)
  starting transfers between devices  9.05 us (6%)
  local copies, waits for them, and re-layouts  7.55 us (5%)
  matrix products  2.47 us (2%)
  other arithmetic  2.33 us (2%)
    unnamed x4, waiting for transfers between devices  36.8 us
    all_gather x1, blocking collectives, body(): lax.all_gather(second_arm, 'row', axis=1, tiled=True)  27 us
    all_gather x1, blocking collectives, body(): lax.all_gather(in_second, 'row', axis=1, tiled=True)  26.6 us
    psum x2, blocking collectives, finish(): lax.psum((jnp.sum(product_sum, axis=0), jnp.sum(product_sum * product_sum...  11.6 us
    ppermute x6, waiting for transfers between devices, prepare(): lax.ppermute(ring[-1], 'ch', [(dev, (dev + 1) % 4) for dev in range(4)])  11.3 us
    unnamed x26, local copies, waits for them, and re-layouts  5.75 us
    all_to_all x1, starting transfers between devices, body(): lax.all_to_all(in_first, 'row', split_axis=2, concat_axis=1, tiled=True)  5.51 us
    ppermute x6, starting transfers between devices, prepare(): lax.ppermute(ring[-1], 'ch', [(dev, (dev + 1) % 4) for dev in range(4)])  3.5 us
  transfers between devices with their start and end apart: 9, of which 7 were waited for; matrix products, arithmetic and copies ran while one was open for 2% of the time, Pallas kernels for 0%

profile of v1, /device:TPU:0, one launch (start us, length us, event | category | flops | bytes accessed | tf_op | source)
XLA Modules:
  0.0 148.3 jit_solution(5572508416028550991)
XLA Ops:
  7.0 0.7 copy-done.9
  7.7 0.7 copy-done.1
  8.4 0.7 copy-done.2
  10.5 2.7 %collective-permute-start.1 = (bf16[32,1,8]{0,2,1:T(8,128)(2,1)S(1)}, bf16[32,1,8]{0,2,1:T(8,128)(2,1)S(1)}, u32[]{:S(2)}, u32[]{:S(2)}) collective-permute-start(bf16[32,1,8]{0,2,1:T(8,128)(2,1)S(1)} %collective-permute-done), channel_id=1, source_target_pairs={{0,1},{1,2},{2,3},{3,0},{4,5},{5,6},{6,7},{7,4},{8,9},{9,10},{10,1... | collective-permute-start | bytes 1544 | tf_op jit(solution)/shard_map/ppermute | solution.py:22
  13.1 0.8 collective-permute-done.1
  14.3 0.7 copy-done.10
  15.5 1.4 collective-permute-done.2
  17.2 0.9 convolution_bitcast_fusion.1
  18.2 27.0 %all_gather.6 = bf16[32,8,8]{0,2,1:T(8,128)(2,1)S(1)} all-gather(bf16[32,1,8]{0,2,1:T(8,128)(2,1)S(1)} %fusion.56), channel_id=1, replica_groups=mesh['row'=8,'ch'=4] {'row'}, dimensions={1}, use_global_device_ids=true | all-gather | bytes 4608 | tf_op jit(solution)/shard_map/all_gather | solution.py:88
  45.5 5.7 %all-reduce.1 = (f32[1,8]{1,0:T(1,128)S(1)}, f32[1,8]{1,0:T(1,128)S(1)}) all-reduce(f32[1,8]{1,0:T(1,128)S(1)} %bitcast.174, f32[1,8]{1,0:T(1,128)S(1)} %bitcast.173), channel_id=1, replica_groups=mesh['row'=8,'ch'=4] {'ch'}, use_global_device_ids=true, to_apply=%region_5.7 | all-reduce | flops 16 | bytes 128 | tf_op jit(solution)/shard_map/psum | solution.py:41
  51.3 0.7 copy.28
  52.1 0.7 compare_convert_fusion
  52.7 18.7 %reduce-scatter.7.cloned.1.call-done = bf16[32,8]{1,0:T(8,128)(2,1)} async-done(((bf16[128,8]{1,0:T(8,128)(2,1)}), bf16[32,8]{1,0:T(8,128)(2,1)}) %reduce-scatter.7.cloned.1.call-update) | async-done | bytes 528
  71.4 0.8 copy.29
  72.4 3.0 %collective-permute-done.3 = bf16[32,1,8]{0,2,1:T(8,128)(2,1)S(1)} collective-permute-done((bf16[32,1,8]{0,2,1:T(8,128)(2,1)S(1)}, bf16[32,1,8]{0,2,1:T(8,128)(2,1)S(1)}, u32[]{:S(2)}, u32[]{:S(2)}) %collective-permute-start.3) | collective-permute-done | bytes 544 | tf_op jit(solution)/shard_map/ppermute | solution.py:22
  75.4 3.0 %collective-permute-done.4 = bf16[32,1,8]{0,2,1:T(8,128)(2,1)S(1)} collective-permute-done((bf16[32,1,8]{0,2,1:T(8,128)(2,1)S(1)}, bf16[32,1,8]{0,2,1:T(8,128)(2,1)S(1)}, u32[]{:S(2)}, u32[]{:S(2)}) %collective-permute-start.4) | collective-permute-done | bytes 544 | tf_op jit(solution)/shard_map/ppermute | solution.py:22
  78.4 3.0 %collective-permute-done.5 = bf16[32,1,8]{0,2,1:T(8,128)(2,1)S(1)} collective-permute-done((bf16[32,1,8]{0,2,1:T(8,128)(2,1)S(1)}, bf16[32,1,8]{0,2,1:T(8,128)(2,1)S(1)}, u32[]{:S(2)}, u32[]{:S(2)}) %collective-permute-start.5) | collective-permute-done | bytes 544 | tf_op jit(solution)/shard_map/ppermute | solution.py:22
  82.5 5.5 %all-to-all-start = ((bf16[32,1,8]{0,1,2:T(2,128)(2,1)}), bf16[32,1,8]{0,1,2:T(2,128)(2,1)S(1)}, u32[]{:S(2)}, u32[]{:S(2)}) async-start(bf16[32,1,8]{0,1,2:T(2,128)(2,1)} %copy.14), calls=%async_computation | async-start | bytes 8192 | tf_op jit(solution)/shard_map/all_to_all | solution.py:97
  88.1 26.6 %all_gather.7 = bf16[32,8,8]{0,2,1:T(8,128)(2,1)S(1)} all-gather(bf16[32,1,8]{0,2,1:T(8,128)(2,1)S(1)} %get-tuple-element.21), channel_id=1, replica_groups=mesh['row'=8,'ch'=4] {'row'}, dimensions={1}, use_global_device_ids=true | all-gather | bytes 4608 | tf_op jit(solution)/shard_map/all_gather | solution.py:102
  114.9 5.9 %all-reduce = (f32[1,8]{1,0:T(1,128)S(1)}, f32[1,8]{1,0:T(1,128)S(1)}) all-reduce(f32[1,8]{1,0:T(1,128)S(1)} %bitcast.176, f32[1,8]{1,0:T(1,128)S(1)} %bitcast.175), channel_id=1, replica_groups=mesh['row'=8,'ch'=4] {'ch'}, use_global_device_ids=true, to_apply=%region_12.14 | all-reduce | flops 16 | bytes 128 | tf_op jit(solution)/shard_map/psum | solution.py:41
  121.0 0.7 copy.30
  121.8 18.1 %reduce-scatter.9.cloned.1.call-done = bf16[32,8]{1,0:T(8,128)(2,1)} async-done(((bf16[128,8]{1,0:T(8,128)(2,1)}), bf16[32,8]{1,0:T(8,128)(2,1)}) %reduce-scatter.9.cloned.1.call-update) | async-done | bytes 528
  139.9 0.8 copy.31
  140.7 0.8 fusion.16
  (55 shorter events, 5.3 us)
Async XLA Ops:
  6.5 64.8 %reduce-scatter.7.cloned.1.call-start = ((), (), s32[]{:S(2)}) async-start(), calls=%async_computation.3 | async-start | bytes 40960
  6.5 3.9 %collective-permute-start = (bf16[32,1,8]{0,2,1:T(8,128)(2,1)}, bf16[32,1,8]{0,2,1:T(8,128)(2,1)S(1)}, u32[]{:S(2)}, u32[]{:S(2)}) collective-permute-start(bf16[32,1,8]{0,2,1:T(8,128)(2,1)} %param.13), channel_id=1, source_target_pairs={{0,1},{1,2},{2,3},{3,0},{4,5},{5,6},{6,7},{7,4},{8,9},{9,10},{10,1... | collective-permute-start | bytes 1544 | tf_op jit(solution)/shard_map/ppermute | solution.py:22
  7.0 0.7 copy-start.9
  7.7 0.7 copy-start.1
  8.4 0.7 copy-start.2
  8.4 0.7 copy-start.3
  9.1 0.7 copy-start.5
  9.1 0.7 copy-start.4
  10.5 3.5 %collective-permute-start.1 = (bf16[32,1,8]{0,2,1:T(8,128)(2,1)S(1)}, bf16[32,1,8]{0,2,1:T(8,128)(2,1)S(1)}, u32[]{:S(2)}, u32[]{:S(2)}) collective-permute-start(bf16[32,1,8]{0,2,1:T(8,128)(2,1)S(1)} %collective-permute-done), channel_id=1, source_target_pairs={{0,1},{1,2},{2,3},{3,0},{4,5},{5,6},{6,7},{7,4},{8,9},{9,10},{10,1... | collective-permute-start | bytes 1544 | tf_op jit(solution)/shard_map/ppermute | solution.py:22
  13.9 3.0 %collective-permute-start.2 = (bf16[32,1,8]{0,2,1:T(8,128)(2,1)S(1)}, bf16[32,1,8]{0,2,1:T(8,128)(2,1)S(1)}, u32[]{:S(2)}, u32[]{:S(2)}) collective-permute-start(bf16[32,1,8]{0,2,1:T(8,128)(2,1)S(1)} %collective-permute-done.1), channel_id=1, source_target_pairs={{0,1},{1,2},{2,3},{3,0},{4,5},{5,6},{6,7},{7,4},{8,9},{9,10},{10,1... | collective-permute-start | bytes 1544 | tf_op jit(solution)/shard_map/ppermute | solution.py:22
  14.3 0.7 copy-start.10
  14.9 2.0 %copy-start = (bf16[32,1,8]{0,2,1:T(8,128)(2,1)S(1)}, bf16[32,1,8]{0,2,1:T(8,128)(2,1)}, u32[]{:S(2)}) copy-start(bf16[32,1,8]{0,2,1:T(8,128)(2,1)} %param.13) | copy-start | bytes 1540
  45.3 5.8 %copy-start.7 = (bf16[2,32,128]{2,1,0:T(8,128)(2,1)S(1)}, bf16[2,32,128]{2,1,0:T(8,128)(2,1)}, u32[]{:S(2)}) copy-start(bf16[2,32,128]{2,1,0:T(8,128)(2,1)} %param.23) | copy-start | bytes 49156
  52.0 20.1 %copy-start.8 = (bf16[2,128,32]{1,2,0:T(8,128)(2,1)S(1)}, bf16[2,128,32]{1,2,0:T(8,128)(2,1)}, u32[]{:S(2)}) copy-start(bf16[2,128,32]{1,2,0:T(8,128)(2,1)} %param.19) | copy-start | bytes 49156
  72.2 9.5 %copy-start.6 = (bf16[2,128,4,32]{1,3,2,0:T(8,128)(2,1)S(1)}, bf16[2,128,4,32]{1,3,2,0:T(8,128)(2,1)}, u32[]{:S(2)}) copy-start(bf16[2,128,4,32]{1,3,2,0:T(8,128)(2,1)} %param.18) | copy-start | bytes 196612
  72.4 3.0 %collective-permute-start.3 = (bf16[32,1,8]{0,2,1:T(8,128)(2,1)S(1)}, bf16[32,1,8]{0,2,1:T(8,128)(2,1)S(1)}, u32[]{:S(2)}, u32[]{:S(2)}) collective-permute-start(bf16[32,1,8]{0,2,1:T(8,128)(2,1)S(1)} %fusion.17), channel_id=1, source_target_pairs={{0,1},{1,2},{2,3},{3,0},{4,5},{5,6},{6,7},{7,4},{8,9},{9,10},{10,1... | collective-permute-start | bytes 1544 | tf_op jit(solution)/shard_map/ppermute | solution.py:22
  75.4 3.0 %collective-permute-start.4 = (bf16[32,1,8]{0,2,1:T(8,128)(2,1)S(1)}, bf16[32,1,8]{0,2,1:T(8,128)(2,1)S(1)}, u32[]{:S(2)}, u32[]{:S(2)}) collective-permute-start(bf16[32,1,8]{0,2,1:T(8,128)(2,1)S(1)} %collective-permute-done.3), channel_id=1, source_target_pairs={{0,1},{1,2},{2,3},{3,0},{4,5},{5,6},{6,7},{7,4},{8,9},{9,10},{10,1... | collective-permute-start | bytes 1544 | tf_op jit(solution)/shard_map/ppermute | solution.py:22
  78.4 3.0 %collective-permute-start.5 = (bf16[32,1,8]{0,2,1:T(8,128)(2,1)S(1)}, bf16[32,1,8]{0,2,1:T(8,128)(2,1)S(1)}, u32[]{:S(2)}, u32[]{:S(2)}) collective-permute-start(bf16[32,1,8]{0,2,1:T(8,128)(2,1)S(1)} %collective-permute-done.4), channel_id=1, source_target_pairs={{0,1},{1,2},{2,3},{3,0},{4,5},{5,6},{6,7},{7,4},{8,9},{9,10},{10,1... | collective-permute-start | bytes 1544 | tf_op jit(solution)/shard_map/ppermute | solution.py:22
  82.5 32.2 %all-to-all-start = ((bf16[32,1,8]{0,1,2:T(2,128)(2,1)}), bf16[32,1,8]{0,1,2:T(2,128)(2,1)S(1)}, u32[]{:S(2)}, u32[]{:S(2)}) async-start(bf16[32,1,8]{0,1,2:T(2,128)(2,1)} %copy.14), calls=%async_computation | async-start | bytes 8192 | tf_op jit(solution)/shard_map/all_to_all | solution.py:97
  88.0 51.9 %reduce-scatter.9.cloned.1.call-start = ((), (), s32[]{:S(2)}) async-start(), calls=%async_computation.4 | async-start | bytes 40960
Sparse Core Ops, SparseCore 0:
  52.2 19.1 reduce-scatter.6
  121.9 17.9 reduce-scatter.8
